TPU v7x, 32 devices: a whole 2x2x4 slice. The times are simulated.
32 devices in a mesh: grp: 2 (over y), theta: 8 (over z, x), phi: 2 (over core).
Axes of the slice: x: 2, y: 2, z: 4, core: 2. Of those that a mesh axis runs over, the one named last changes fastest.
Arguments:
- maps: bfloat16 [8, 4096, 4096], P('grp', 'theta', 'phi'), parts along dimension 0, may hold values from -6 to 6
- deltas: bfloat16 [4096, 4, 4096], P('phi', None, 'theta'), may hold values from -1 to 1
- spin_rows: bfloat16 [4096, 2, 4], P('phi'), may hold values from -1 to 1
- ell_index: int32 [4], replicated, may hold values from 1024 to 2047
- owner_map: int32 [4096], replicated, may hold values from 0 to 4095, each once
- prior: float32 [4], replicated, may hold values from 0.3 to 3
Outputs:
- gradient: float32 [8, 2, 4096], P('grp', None, ('theta', 'phi')), parts along dimension 0
There are 2 independent parts, one for each index of `grp`. A program takes and returns all parts, laid end to end along the dimension named above; an argument that names none is the same for every part. Nothing has to cross between parts.
Inputs may be any that keep to these rules, and one draw needn't show every extreme that they name: `ell_index`: every selected degree is at least 1024; tables may repeat a degree. A permutation of the Fourier indices; slot s of deltas and of the output belongs to the frequency owner_map[s].
All inputs are finite; a program needn't handle non-finite values.
Results may differ from a plain program's by a relative error of at most 0.0003.
Values may be sent and summed in bfloat16 or wider, within the bound.
No kernel may reach another device: no remote copies, remote signals or barrier semaphores. Data moves between devices by JAX's collectives and lax.ppermute only.
A program may use at most 256 MiB of HBM per device.

v0:
```python
import math

import jax
import jax.numpy as jnp
from jax import lax
from jax.sharding import PartitionSpec as P


def exact_einsum(form, table, operand):
    return jnp.einsum(form, table, operand, precision=lax.Precision.HIGHEST)


def angle_tables(row_count, start, count, modulus):
    freq_rows = jnp.arange(row_count, dtype=jnp.int32)
    sample_cols = start + jnp.arange(count, dtype=jnp.int32)
    angles = (
        2.0
        * math.pi
        / modulus
        * jnp.mod(freq_rows[:, None] * sample_cols[None, :], modulus).astype(jnp.float32)
    )
    return (jnp.cos(angles), jnp.sin(angles))


def row_transform(real_part, imag_part, outer_len, inner_len):
    row_count = real_part.shape[0]
    length = outer_len * inner_len
    cos_a, sin_a = angle_tables(outer_len, 0, outer_len, outer_len)
    real_blocks = real_part.reshape(row_count, outer_len, inner_len)
    section_real = exact_einsum("ka,rab->rkb", cos_a, real_blocks)
    section_imag = -exact_einsum("ka,rab->rkb", sin_a, real_blocks)
    if imag_part is not None:
        imag_blocks = imag_part.reshape(row_count, outer_len, inner_len)
        section_real = section_real + exact_einsum("ka,rab->rkb", sin_a, imag_blocks)
        section_imag = section_imag + exact_einsum("ka,rab->rkb", cos_a, imag_blocks)
    cos_t, sin_t = angle_tables(outer_len, 0, inner_len, length)
    turned_real = section_real * cos_t + section_imag * sin_t
    turned_imag = section_imag * cos_t - section_real * sin_t
    cos_b, sin_b = angle_tables(inner_len, 0, inner_len, inner_len)
    out_real = exact_einsum("qb,rkb->rqk", cos_b, turned_real) + exact_einsum(
        "qb,rkb->rqk", sin_b, turned_imag
    )
    out_imag = exact_einsum("qb,rkb->rqk", cos_b, turned_imag) - exact_einsum(
        "qb,rkb->rqk", sin_b, turned_real
    )
    return (out_real.reshape(row_count, length), out_imag.reshape(row_count, length))


def column_transform(real_part, imag_part, outer_len, inner_len, start):
    fields = real_part.shape[0]
    count = real_part.shape[2]
    slots = real_part.shape[3]
    length = outer_len * inner_len
    cos_a, sin_a = angle_tables(outer_len, 0, outer_len, outer_len)
    section_real = exact_einsum("ka,fabm->fkbm", cos_a, real_part) + exact_einsum(
        "ka,fabm->fkbm", sin_a, imag_part
    )
    section_imag = exact_einsum("ka,fabm->fkbm", cos_a, imag_part) - exact_einsum(
        "ka,fabm->fkbm", sin_a, real_part
    )
    cos_t, sin_t = angle_tables(outer_len, start, count, length)
    cos_t = cos_t[:, :, None]
    sin_t = sin_t[:, :, None]
    turned_real = section_real * cos_t + section_imag * sin_t
    turned_imag = section_imag * cos_t - section_real * sin_t
    cos_b, sin_b = angle_tables(inner_len, start, count, inner_len)
    out_real = exact_einsum("qb,fkbm->fqkm", cos_b, turned_real) + exact_einsum(
        "qb,fkbm->fqkm", sin_b, turned_imag
    )
    out_imag = exact_einsum("qb,fkbm->fqkm", cos_b, turned_imag) - exact_einsum(
        "qb,fkbm->fqkm", sin_b, turned_real
    )
    return (out_real.reshape(fields, length, slots), out_imag.reshape(fields, length, slots))


def accumulate(spectrum_block, table_block, spin_block, length, ell_index):
    count = table_block.shape[0]
    positions = jnp.arange(count, dtype=jnp.int32)
    freq = jnp.where(positions < length // 2, positions, positions - length)
    terms = []
    for degree in range(table_block.shape[1]):
        keep_rows = (jnp.abs(freq) <= ell_index[degree]).astype(jnp.float32)
        row_weights = spin_block[:, :, degree].astype(jnp.float32).T * keep_rows[None, :]
        table = table_block[:, degree, :].astype(jnp.float32)
        terms.append(
            jnp.einsum(
                "fk,ks,xfks->fxs",
                row_weights,
                table,
                spectrum_block,
                precision=lax.Precision.HIGHEST,
            )
        )
    return jnp.stack(terms)


def on_device(maps, deltas, spin_rows, ell_index, owner_map, prior):
    theta_count = lax.axis_size("theta")
    phi_count = lax.axis_size("phi")
    length = maps.shape[2] * phi_count
    values = maps.astype(jnp.float32)
    planes = jnp.stack([values[0], values[1] * values[2], values[1] * values[3]])
    row_planes = lax.all_to_all(planes, "phi", split_axis=1, concat_axis=2, tiled=True)
    inner_len = length // theta_count
    spectra = [
        row_transform(row_planes[0], None, theta_count, inner_len),
        row_transform(row_planes[1], row_planes[2], theta_count, inner_len),
    ]
    stacked = jnp.stack(
        [
            jnp.stack([spectrum[0] for spectrum in spectra]),
            jnp.stack([spectrum[1] for spectrum in spectra]),
        ]
    )
    permuted = jnp.take(stacked, owner_map, axis=3)
    columns = lax.all_to_all(permuted, "theta", split_axis=3, concat_axis=2, tiled=True)
    fields = columns.shape[1]
    slots = columns.shape[3]
    sub_rows = columns.shape[2] // theta_count
    blocks = columns.reshape(2, fields, theta_count, sub_rows, slots)
    row_start = lax.axis_index("phi") * sub_rows
    spec_real, spec_imag = column_transform(blocks[0], blocks[1], theta_count, inner_len, row_start)
    combined = jnp.stack([spec_real, spec_imag])
    totals = accumulate(
        combined,
        lax.all_gather(deltas, "phi", axis=0, tiled=True),
        lax.all_gather(spin_rows, "phi", axis=0, tiled=True),
        length,
        ell_index,
    )
    shares = lax.psum_scatter(totals, "phi", scatter_dimension=3, tiled=True)
    share_count = shares.shape[3]
    slot_start = lax.axis_index("theta") * slots + lax.axis_index("phi") * share_count
    share_ids = lax.dynamic_slice_in_dim(owner_map, slot_start, share_count)
    slot_freq = jnp.where(share_ids < length // 2, share_ids, share_ids - length)
    ell_float = ell_index.astype(jnp.float32)
    weight = 2.0 * math.pi / length * jnp.sqrt((2.0 * ell_float + 1.0) / (4.0 * math.pi)) / length
    keep_slots = (jnp.abs(slot_freq)[None, :] <= ell_index[:, None]).astype(jnp.float32) * weight[
        :, None
    ]
    scalar_real = shares[:, 0, 0] * keep_slots
    scalar_imag = shares[:, 0, 1] * keep_slots
    spin_real = shares[:, 1, 0] * keep_slots
    spin_imag = shares[:, 1, 1] * keep_slots
    coupling = (prior * jnp.sqrt(ell_float * (ell_float + 1.0)) / (length // 2))[:, None]
    inner_real = -spin_imag - coupling * scalar_real
    inner_imag = spin_real - coupling * scalar_imag
    turns = jnp.mod(-slot_freq, 4)
    phase_real = jnp.where(turns == 0, 1.0, jnp.where(turns == 2, -1.0, 0.0)).astype(jnp.float32)[
        None, :
    ]
    phase_imag = jnp.where(turns == 1, 1.0, jnp.where(turns == 3, -1.0, 0.0)).astype(jnp.float32)[
        None, :
    ]
    out_real = phase_real * inner_real - phase_imag * inner_imag
    out_imag = phase_real * inner_imag + phase_imag * inner_real
    return jnp.stack([out_real, out_imag], axis=1)


def solution(mesh):
    placed = (
        P("grp", "theta", "phi"),
        P("phi", None, "theta"),
        P("phi", None, None),
        P(),
        P(),
        P(),
    )
    return jax.shard_map(
        on_device,
        mesh=mesh,
        in_specs=placed,
        out_specs=P("grp", None, ("theta", "phi")),
        check_vma=False,
    )
```

profile of v0, /device:TPU:11, one launch (start us, length us, event | category | flops | bytes accessed | tf_op | source)
XLA Modules:
  0.0 1104.7 jit_solution(13020259938788177995)
XLA Ops:
  6.5 11.3 %convert_element_type.145 = f32[4,512,2048]{2,1,0:T(8,128)} convert(bf16[4,512,2048]{2,1,0:T(8,128)(2,1)} %param.6) | non-fusion elementwise | flops 4194304 | bytes 25165824 | tf_op jit(solution)/shard_map/convert_element_type | solution.py:101
  40.1 16.7 %copy.115 = f32[3,512,2048]{2,0,1:T(4,128)S(1)} copy(f32[3,512,2048]{2,1,0:T(8,128)} %pad_maximum_fusion.1) | data formatting | bytes 25165824 | tf_op jit(solution)/shard_map/stack | solution.py:102
  56.8 17.7 %all_to_all.30 = f32[3,512,2048]{2,0,1:T(4,128)S(1)} all-to-all(f32[3,512,2048]{2,0,1:T(4,128)S(1)} %copy.115), channel_id=1, replica_groups=mesh['grp'=2,'theta'=8,'phi'=2] {'phi'}, dimensions={1} | all-to-all | bytes 25165824 | tf_op jit(solution)/shard_map/all_to_all | solution.py:103
  74.5 14.4 %copy.241 = f32[3,2,256,2048]{3,1,2,0:T(2,128)} copy(f32[3,2,256,2048]{3,0,2,1:T(4,128)S(1)} %bitcast.262) | data formatting | bytes 25165824 | tf_op jit(solution)/shard_map/all_to_all | solution.py:103
  155.8 10.5 fusion.24
  166.2 13.1 %fusion.36 = f32[256,8,512]{2,0,1:T(8,128)S(1)} fusion(f32[256,8,512]{2,1,0:T(8,128)S(1)} %get-tuple-element.26), kind=kOutput, calls=%fused_computation.77 | convolution fusion | flops 6446120960 | bytes 8388608 | tf_op jit(solution)/shard_map/qb,rkb->rqk/dot_general | solution.py:10
  179.3 15.6 %fusion.34 = f32[256,8,512]{2,0,1:T(8,128)} fusion(f32[256,8,512]{2,1,0:T(8,128)S(1)} %get-tuple-element.26), kind=kOutput, calls=%fused_computation.75 | convolution fusion | flops 6446120960 | bytes 8388608 | tf_op jit(solution)/shard_map/qb,rkb->rqk/dot_general | solution.py:10
  194.9 15.8 %fusion.28 = f32[256,8,512]{2,0,1:T(8,128)} fusion(f32[256,8,512]{2,1,0:T(8,128)S(1)} %get-tuple-element.37), kind=kOutput, calls=%fused_computation.69 | convolution fusion | flops 6446120960 | bytes 8388608 | tf_op jit(solution)/shard_map/qb,rkb->rqk/dot_general | solution.py:10
  210.7 16.0 %fusion.26 = f32[256,8,512]{2,0,1:T(8,128)} fusion(f32[256,8,512]{2,1,0:T(8,128)S(1)} %get-tuple-element.37), kind=kOutput, calls=%fused_computation.67 | convolution fusion | flops 6446120960 | bytes 8388608 | tf_op jit(solution)/shard_map/qb,rkb->rqk/dot_general | solution.py:10
  226.7 15.9 %add_bitcast_fusion.2 = f32[256,512,8]{1,0,2:T(8,128)} fusion(f32[256,8,512]{2,0,1:T(8,128)S(1)} %fusion.36, f32[256,8,512]{2,1,0:T(8,128)S(1)} %get-tuple-element.25), kind=kOutput, calls=%fused_computation.66 | convolution fusion | flops 6447169536 | bytes 12582912 | tf_op jit(solution)/shard_map/qb,rkb->rqk/dot_general | solution.py:10
  257.6 15.8 %add_bitcast_fusion.1 = f32[256,512,8]{1,0,2:T(8,128)} fusion(f32[256,8,512]{2,0,1:T(8,128)S(1)} %copy-done.13, f32[256,8,512]{2,1,0:T(8,128)S(1)} %copy-done.4), kind=kOutput, calls=%fused_computation.64 | convolution fusion | flops 6447169536 | bytes 12582912 | tf_op jit(solution)/shard_map/qb,rkb->rqk/dot_general | solution.py:10
  288.3 16.1 %subtract_bitcast_fusion.2 = f32[256,512,8]{1,0,2:T(8,128)} fusion(f32[256,8,512]{2,0,1:T(8,128)S(1)} %copy-done.12, f32[256,8,512]{2,1,0:T(8,128)S(1)} %copy-done.7), kind=kOutput, calls=%fused_computation.63 | convolution fusion | flops 6447169536 | bytes 12582912 | tf_op jit(solution)/shard_map/qb,rkb->rqk/dot_general | solution.py:10
  319.4 15.8 %subtract_bitcast_fusion.1 = f32[256,512,8]{1,0,2:T(8,128)} fusion(f32[256,8,512]{2,0,1:T(8,128)S(1)} %copy-done.11, f32[256,8,512]{2,1,0:T(8,128)S(1)} %copy-done.5), kind=kOutput, calls=%fused_computation.62 | convolution fusion | flops 6447169536 | bytes 12582912 | tf_op jit(solution)/shard_map/qb,rkb->rqk/dot_general | solution.py:10
  372.7 52.5 %gather_fusion = f32[4096,2,2,256]{3,2,1,0:T(2,128)} fusion(f32[2,2,256,4096]{2,1,3,0:T(2,128)} %pad_maximum_fusion, s32[4096]{0:T(1024)S(1)} %fusion.105), kind=kCustom, calls=%fused_computation | custom fusion | bytes 33570816 | tf_op jit(solution)/shard_map/jit(_take)/gather | solution.py:115
  425.2 17.6 %select_bitcast_fusion = f32[2,2,256,4096]{2,1,0,3:T(2,128)} fusion(f32[4096,2,2,256]{3,2,1,0:T(2,128)} %gather_fusion, pred[4096]{0:T(1024)(128)(4,1)S(1)} %compare_and_fusion), kind=kLoop, calls=%fused_computation.9 | loop fusion | flops 4194304 | bytes 33558528 | tf_op jit(solution)/shard_map/jit(_take)/select_n | solution.py:115
  472.1 16.9 %all-gather.2.cloned.1.call-done = bf16[4096,4,512]{2,0,1:T(8,128)(2,1)} async-done(((bf16[2048,4,512]{2,0,1:T(8,128)(2,1)}), bf16[4096,4,512]{2,0,1:T(8,128)(2,1)}) %all-gather.2.cloned.1.call-update) | async-done | bytes 16777232 | tf_op jit(solution)/shard_map/all_gather | solution.py:126
  489.0 15.4 %fusion.18 = (f32[4096,512]{1,0:T(8,128)}, f32[4096,512]{1,0:T(8,128)}, f32[4096,512]{1,0:T(8,128)}, f32[4096,512]{1,0:T(8,128)}) fusion(bf16[4096,4,512]{2,0,1:T(8,128)(2,1)} %all-gather.2.cloned.1.call-done), kind=kLoop, calls=%fused_computation.41 | loop fusion | flops 8388608 | bytes 50331648 | tf_op jit(solution)/shard_map/convert.15
  504.4 20.2 %multiply_bitcast_fusion = (f32[2,512,4096]{1,0,2:T(2,128)}, f32[2,512,4096]{1,0,2:T(2,128)}) fusion(f32[4096,512]{1,0:T(8,128)} %get-tuple-element.16, f32[4096,2]{1,0:T(8,128)} %copy.144, f32[4096,512]{1,0:T(8,128)} %get-tuple-element.17, f32[4096,2]{1,0:T(8,128)S(1)} %copy.143), kind=kLoop, calls=%fused_computation.10 | loop fusion | flops 8388608 | bytes 50397184
  524.6 15.2 %copy.190 = f32[2,512,4096]{1,2,0:T(8,128)} copy(f32[2,512,4096]{1,0,2:T(2,128)} %get-tuple-element.48) | data formatting | bytes 33554432
  549.9 20.1 %multiply_bitcast_fusion.2 = (f32[2,512,4096]{1,0,2:T(2,128)}, f32[2,512,4096]{1,0,2:T(2,128)}) fusion(f32[4096,512]{1,0:T(8,128)} %get-tuple-element.18, f32[4096,2]{1,0:T(8,128)} %copy.142, f32[4096,512]{1,0:T(8,128)} %get-tuple-element.19, f32[4096,2]{1,0:T(8,128)S(1)} %copy-done.18), kind=kLoop, calls=%fused_computation.12 | loop fusion | flops 8388608 | bytes 50397184
  570.1 15.2 %copy.188 = f32[2,512,4096]{1,2,0:T(8,128)} copy(f32[2,512,4096]{1,0,2:T(2,128)} %get-tuple-element.50) | data formatting | bytes 33554432
  595.4 213.4 %all-to-all-done.1 = f32[2,2,256,4096]{2,1,0,3:T(2,128)} async-done(((f32[2,2,256,4096]{2,1,0,3:T(2,128)}), f32[2,2,256,4096]{2,1,0,3:T(2,128)}, u32[]{:S(2)}, u32[]{:S(2)}) %all-to-all-start.1) | async-done | bytes 16777248 | tf_op jit(solution)/shard_map/all_to_all | solution.py:116
  808.8 19.4 %copy.177 = f32[2,2,256,8,512]{4,3,2,1,0:T(8,128)} copy(f32[2,2,256,8,512]{2,1,0,4,3:T(2,128)} %bitcast.33) | data formatting | bytes 33554432 | tf_op jit(solution)/shard_map/all_to_all | solution.py:116
  828.1 11.8 %fusion.2 = f32[2,256,512,8]{2,3,1,0:T(8,128)} fusion(f32[2,2,8,256,512]{4,2,3,1,0:T(8,128)} %bitcast.258), kind=kOutput, calls=%fused_computation.28 | convolution fusion | flops 201327488 | bytes 16777216 | tf_op jit(solution)/shard_map/ka,fabm->fkbm/dot_general | solution.py:10
  858.8 21.9 %fusion = (f32[2,8,256,512]{3,1,2,0:T(8,128)}, f32[2,8,256,512]{3,1,2,0:T(8,128)}) fusion(f32[8,256]{0,1:T(8,128)S(1)} %copy.135, f32[8,256]{0,1:T(8,128)S(1)} %copy.134, f32[2,256,512,8]{2,3,1,0:T(8,128)} %fusion.2, f32[2,256,512,8]{2,3,1,0:T(8,128)} %fusion.3, f32[2,256,512,8]{2,3,1,0:T(8,128)} %fusion.5, f32[2,2,8,256,512]{4,2,3,1,0:T(8,128)} %bitcast.259), kind=kOutput, calls=%fused_computation.24 | convolution fusion | flops 218104704 | bytes 50348032 | tf_op jit(solution)/shard_map/ka,fabm->fkbm/dot_general | solution.py:10
  880.7 26.0 %fusion.8 = f32[2,8,512,512]{2,3,1,0:T(8,128)} fusion(f32[2,8,256,512]{3,1,2,0:T(8,128)} %get-tuple-element.15, s32[256]{0:T(256)S(1)} %iota_add_fusion), kind=kOutput, calls=%fused_computation.34 | convolution fusion | flops 12886736896 | bytes 25166848 | tf_op jit(solution)/shard_map/qb,fkbm->fqkm/dot_general | solution.py:10
  906.7 25.8 %fusion.6 = f32[2,8,512,512]{2,3,1,0:T(8,128)S(1)} fusion(f32[2,8,256,512]{3,1,2,0:T(8,128)} %get-tuple-element.15, s32[256]{0:T(256)S(1)} %iota_add_fusion), kind=kOutput, calls=%fused_computation.32 | convolution fusion | flops 12886736896 | bytes 25166848 | tf_op jit(solution)/shard_map/qb,fkbm->fqkm/dot_general | solution.py:10
  932.5 49.7 %add_bitcast_fusion = f32[2,512,8,512]{3,1,2,0:T(8,128)} fusion(f32[2,8,512,512]{2,3,1,0:T(8,128)} %fusion.8, f32[2,8,256,512]{3,1,2,0:T(8,128)} %get-tuple-element.14, s32[256]{0:T(256)S(1)} %iota_add_fusion), kind=kOutput, calls=%fused_computation.14 | convolution fusion | flops 12890931200 | bytes 41944064 | tf_op jit(solution)/shard_map/qb,fkbm->fqkm/dot_general | solution.py:10
  982.2 17.7 %copy.240 = f32[2,512,8,512]{3,2,1,0:T(8,128)} copy(f32[2,512,8,512]{3,1,2,0:T(8,128)} %add_bitcast_fusion) | data formatting | bytes 33554432 | tf_op jit(solution)/shard_map/add | solution.py:67
  1000.0 27.7 %subtract_bitcast_fusion = f32[2,512,8,512]{3,1,2,0:T(8,128)} fusion(f32[2,8,512,512]{2,3,1,0:T(8,128)S(1)} %fusion.6, f32[2,8,256,512]{3,1,2,0:T(8,128)} %get-tuple-element.14, s32[256]{0:T(256)S(1)} %iota_add_fusion), kind=kOutput, calls=%fused_computation.13 | convolution fusion | flops 12890931200 | bytes 41944064 | tf_op jit(solution)/shard_map/qb,fkbm->fqkm/dot_general | solution.py:10
  1027.7 19.3 %copy.239 = f32[2,512,8,512]{3,2,1,0:T(8,128)} copy(f32[2,512,8,512]{3,1,2,0:T(8,128)} %subtract_bitcast_fusion) | data formatting | bytes 33554432 | tf_op jit(solution)/shard_map/sub | solution.py:70
  1047.0 27.6 %multiply_reduce_fusion.3 = (f32[2,512,2]{1,0,2:T(2,128)S(1)}, f32[2,512,2]{1,0,2:T(2,128)S(1)}, f32[2,512,2]{1,0,2:T(2,128)S(1)}, f32[2,512,2]{1,0,2:T(2,128)S(1)}) fusion(f32[2,512,4096]{1,2,0:T(8,128)} %copy.188, f32[1,2,4096,512]{3,2,1,0:T(8,128)} %bitcast.264, f32[1,2,4096,512]{3,2,1,0:T(8,128)S(1)} %bitcast.263, f32[2,512,4096]{1,2,0:T(8,128)} %copy.189, ...), kind=kLoop, calls=%fused_computation.5 | loop fusion | flops 75489280 | bytes 100696064 | tf_op jit(solution)/shard_map/fk,ks,xfks->fxs/dot_general | solution.py:86
  (128 shorter events, 262.6 us)
Async XLA Ops:
  104.3 8.7 copy-start.10
  124.9 10.2 copy-start.8
  125.0 10.2 copy-start.14
  147.1 8.6 copy-start.9
  166.2 60.5 %copy-start.6 = (f32[256,8,512]{2,1,0:T(8,128)}, f32[256,8,512]{2,1,0:T(8,128)S(1)}, u32[]{:S(2)}) copy-start(f32[256,8,512]{2,1,0:T(8,128)S(1)} %get-tuple-element.25) | copy-start | bytes 12582916
  194.9 31.8 %copy-start.19 = (s32[4096]{0:T(1024)S(1)}, s32[4096]{0:T(1024)}, u32[]{:S(2)}) copy-start(s32[4096]{0:T(1024)} %param.10) | copy-start | bytes 49156
  248.1 9.5 copy-start.4
  248.1 9.5 copy-start.13
  278.9 9.5 copy-start.7
  278.9 9.5 copy-start.12
  309.9 9.5 copy-start.5
  309.9 9.5 copy-start.11
  340.7 7.9 copy-start.15
  340.7 7.9 copy-start.16
  348.6 7.7 copy-start.17
  442.8 366.0 %all-to-all-start.1 = ((f32[2,2,256,4096]{2,1,0,3:T(2,128)}), f32[2,2,256,4096]{2,1,0,3:T(2,128)}, u32[]{:S(2)}, u32[]{:S(2)}) async-start(f32[2,2,256,4096]{2,1,0,3:T(2,128)} %select_bitcast_fusion), calls=%async_computation.1 | async-start | bytes 33554432 | tf_op jit(solution)/shard_map/all_to_all | solution.py:116
  448.6 40.4 %all-gather.2.cloned.1.call-start = ((), (), s32[]{:S(2)}) async-start(), calls=%async_computation.3 | async-start | bytes 25165824 | tf_op jit(solution)/shard_map/all_gather | solution.py:126
  457.0 0.8 copy-start.20
  457.0 3.0 copy-start.21
  457.0 14.5 %copy-start.27 = (f32[4]{0:T(128)S(1)}, f32[4]{0:T(128)}, u32[]{:S(2)}) copy-start(f32[4]{0:T(128)} %param.11) | copy-start | bytes 52
  457.0 632.9 %reduce-scatter.4.cloned.1.call-start = ((), (), s32[]{:S(2)}) async-start(), calls=%async_computation.4 | async-start | bytes 393216
  524.6 16.5 %copy-start.1 = (f32[2,512,4096]{1,0,2:T(2,128)S(1)}, f32[2,512,4096]{1,0,2:T(2,128)}, u32[]{:S(2)}) copy-start(f32[2,512,4096]{1,0,2:T(2,128)} %get-tuple-element.47) | copy-start | bytes 50331652
  541.1 8.9 copy-start.18
  570.1 16.5 %copy-start.2 = (f32[2,512,4096]{1,0,2:T(2,128)S(1)}, f32[2,512,4096]{1,0,2:T(2,128)}, u32[]{:S(2)}) copy-start(f32[2,512,4096]{1,0,2:T(2,128)} %get-tuple-element.49) | copy-start | bytes 50331652
  828.1 11.8 %copy-start = (f32[2,2,256,8,512]{4,3,2,1,0:T(8,128)S(1)}, f32[2,2,256,8,512]{4,3,2,1,0:T(8,128)}, u32[]{:S(2)}) copy-start(f32[2,2,256,8,512]{4,3,2,1,0:T(8,128)} %copy.177) | copy-start | bytes 50331652
  1027.7 19.4 %copy-start.3 = (f32[2,512,8,512]{3,2,1,0:T(8,128)S(1)}, f32[2,512,8,512]{3,2,1,0:T(8,128)}, u32[]{:S(2)}) copy-start(f32[2,512,8,512]{3,2,1,0:T(8,128)} %copy.240) | copy-start | bytes 50331652
  1074.6 22.2 %copy-start.22 = (s32[4]{0:T(128)S(1)}, s32[4]{0:T(128)}, u32[]{:S(2)}) copy-start(s32[4]{0:T(128)} %param.9) | copy-start | bytes 52
  1074.7 22.2 %copy-start.23 = (f32[256]{0:T(256)S(1)}, f32[256]{0:T(256)}, u32[]{:S(2)}) copy-start(f32[256]{0:T(256)} %get-tuple-element.12) | copy-start | bytes 3076
  1074.7 22.2 %copy-start.24 = (f32[256]{0:T(256)S(1)}, f32[256]{0:T(256)}, u32[]{:S(2)}) copy-start(f32[256]{0:T(256)} %compare_select_fusion.7) | copy-start | bytes 3076
  1074.7 22.2 %copy-start.25 = (f32[4]{0:T(128)S(1)}, f32[4]{0:T(128)}, u32[]{:S(2)}) copy-start(f32[4]{0:T(128)} %get-tuple-element.41) | copy-start | bytes 52
  1074.7 22.2 %copy-start.26 = (f32[4]{0:T(128)S(1)}, f32[4]{0:T(128)}, u32[]{:S(2)}) copy-start(f32[4]{0:T(128)} %get-tuple-element.42) | copy-start | bytes 52
Sparse Core Ops, SparseCore 0:
  457.2 31.7 all-gather.1
  1079.6 10.3 reduce-scatter.3
where the time goes:
time: 1110 us; the launch traced here: 1100 us
  matrix products  354 us (32%)
  local copies, waits for them, and re-layouts  310 us (28%)
  waiting for transfers between devices  240 us (22%)
  other arithmetic  161 us (15%)
  blocking collectives  19.9 us (2%)
  between operations  14.1 us (1%)
    dot_general x22, matrix products, exact_einsum(): return jnp.einsum(form, table, operand, precision=lax.Precision.HIGHEST)  354 us
    all_to_all x1, waiting for transfers between devices, on_device(): lax.all_to_all(permuted, 'theta', split_axis=3, concat_axis=2, tiled=True)  213 us
    unnamed x68, local copies, waits for them, and re-layouts  68.2 us
    gather x1, local copies, waits for them, and re-layouts, on_device(): permuted = jnp.take(stacked, owner_map, axis=3)  52.5 us
    unnamed x2, other arithmetic  40.3 us
    dot_general x1, other arithmetic, accumulate(): jnp.einsum('fk,ks,xfks->fxs', row_weights, table, spectrum_block, precisi...  27.6 us
    another operation x3, other arithmetic, on_device(): jnp.stack([jnp.stack([spectrum[0] for spectrum in spectra]), jnp.stack([s...  24 us
  transfers between devices with their start and end apart: 3, of which 3 were waited for; matrix products, arithmetic and copies ran while one was open for 11% of the time, Pallas kernels for 0%

commit v1 on v0

v1 whole, which is shorter than its diff:
```python
import functools
import math

import jax
import jax.numpy as jnp
import numpy as np
from jax import lax
from jax.experimental import pallas as pl
from jax.experimental.pallas import tpu as pltpu
from jax.sharding import PartitionSpec as P

RADIX = 16
LINK_SCALE = 0.25
LINK_TYPE = jnp.float16
VMEM_BYTES = 56 * 1024 * 1024


def add(x, y):
    return y if x is None else x if y is None else x + y


def sub(x, y):
    return x if y is None else -y if x is None else x - y


def dft4(x0, x1, x2, x3):
    s02 = (add(x0[0], x2[0]), add(x0[1], x2[1]))
    d02 = (sub(x0[0], x2[0]), sub(x0[1], x2[1]))
    s13 = (add(x1[0], x3[0]), add(x1[1], x3[1]))
    d13 = (sub(x1[0], x3[0]), sub(x1[1], x3[1]))
    return (
        (add(s02[0], s13[0]), add(s02[1], s13[1])),
        (add(d02[0], d13[1]), sub(d02[1], d13[0])),
        (sub(s02[0], s13[0]), sub(s02[1], s13[1])),
        (sub(d02[0], d13[1]), add(d02[1], d13[0])),
    )


def turn(x, power):
    re, im = x
    if power == 0:
        return x
    if power == 4:
        return (im, None if re is None else -re)
    c = math.cos(2 * math.pi * power / RADIX)
    s = math.sin(2 * math.pi * power / RADIX)
    if im is None:
        return (re * c, re * (-s))
    if re is None:
        return (im * s, im * c)
    return (re * c + im * s, im * c - re * s)


def dft16(xs):
    inner = [dft4(xs[a], xs[a + 4], xs[a + 8], xs[a + 12]) for a in range(4)]
    out = [None] * RADIX
    for low in range(4):
        turned = [turn(inner[a][low], a * low) for a in range(4)]
        for high, value in enumerate(dft4(*turned)):
            out[low + 4 * high] = value
    return out


def split_store(hi_ref, lo_ref, k, rows, lanes, value):
    hi = value.astype(jnp.bfloat16)
    hi_ref[k, rows, lanes] = hi
    lo_ref[k, rows, lanes] = (value - hi.astype(jnp.float32)).astype(jnp.bfloat16)


def first_stage(load, turn_ref, hi_ref, lo_ref, row_total, inner):
    step = 16
    width = min(128, inner)

    def body(i, carry):
        rows = pl.ds(pl.multiple_of(i * step, step), step)
        for lane in range(0, inner, width):
            xs = [load(a, rows, lane, width) for a in range(RADIX)]
            ys = dft16(xs)
            for k in range(RADIX):
                re, im = ys[k]
                if k:
                    c = turn_ref[0, k : k + 1, lane : lane + width]
                    s = turn_ref[1, k : k + 1, lane : lane + width]
                    if im is None:
                        re, im = re * c, -re * s
                    else:
                        re, im = re * c + im * s, im * c - re * s
                if im is None:
                    im = jnp.zeros_like(re)
                split_store(hi_ref, lo_ref, k, rows, pl.ds(lane, width), re)
                split_store(hi_ref, lo_ref, k, rows, pl.ds(inner + lane, width), im)
        return carry

    lax.fori_loop(0, row_total // step, body, 0)


def second_stage(k, w_ref, hi_ref, lo_ref):
    dims = (((1,), (1,)), ((), ()))
    hi = hi_ref[k]
    lo = lo_ref[k]
    dot = functools.partial(lax.dot_general, dimension_numbers=dims, preferred_element_type=jnp.float32)
    return dot(w_ref[0], hi) + dot(w_ref[0], lo) + dot(w_ref[1], hi)


def front_kernel(rows_ref, w_ref, turn_ref, *refs, spin):
    planes = refs[: 3 if spin else 1]
    out_ref, hi_ref, lo_ref, spec_ref = refs[len(planes) :]
    halves, _, row_total, _ = planes[0].shape
    inner = w_ref.shape[1] // 2
    per_half = RADIX // halves

    def load(a, rows, lane, width):
        half, start = a // per_half, (a % per_half) * inner + lane
        read = lambda plane: planes[plane][half, 0, rows, pl.ds(start, width)].astype(jnp.float32)
        if not spin:
            return (read(0), None)
        base = read(0)
        return (base * read(1), base * read(2))

    first_stage(load, turn_ref, hi_ref, lo_ref, row_total, inner)

    def body(k, carry):
        g = second_stage(k, w_ref, hi_ref, lo_ref)
        start = pl.multiple_of(k * inner, inner)
        spec_ref[pl.ds(start, inner), :row_total] = g[:inner] * LINK_SCALE
        spec_ref[pl.ds(start, inner), row_total:] = g[inner:] * LINK_SCALE
        return carry

    lax.fori_loop(0, RADIX, body, 0)

    def gather(i, carry):
        base = pl.multiple_of(i * 16, 16)
        for u in range(16):
            out_ref[pl.ds(base + u, 1), :] = spec_ref[pl.ds(rows_ref[base + u], 1), :]
        return carry

    lax.fori_loop(0, out_ref.shape[0] // 16, gather, 0)


def front(maps, w, turns, source_rows, spin):
    halves, _, row_total, half_cols = maps.shape
    picks = (1, 2, 3) if spin else (0,)
    inner = w.shape[1] // 2
    length = RADIX * inner
    vmem = pl.BlockSpec(memory_space=pltpu.VMEM)
    plane_specs = [
        pl.BlockSpec((halves, 1, row_total, half_cols), functools.partial(lambda p, i: (0, p, 0, 0), p))
        for p in picks
    ]
    return pl.pallas_call(
        functools.partial(front_kernel, spin=spin),
        grid=(1,),
        in_specs=[pl.BlockSpec(memory_space=pltpu.SMEM), vmem, vmem, *plane_specs],
        out_specs=vmem,
        out_shape=jax.ShapeDtypeStruct((length, 2 * row_total), jnp.float32),
        scratch_shapes=[
            pltpu.VMEM((RADIX, row_total, 2 * inner), jnp.bfloat16),
            pltpu.VMEM((RADIX, row_total, 2 * inner), jnp.bfloat16),
            pltpu.VMEM((length, 2 * row_total), jnp.float32),
        ],
        compiler_params=pltpu.CompilerParams(vmem_limit_bytes=VMEM_BYTES),
    )(source_rows, w, turns, *([maps] * len(picks)))


def back_kernel(code_ref, w_ref, turn_ref, weight_ref, table_ref, out_ref, hi_ref, lo_ref, g_ref):
    slots = code_ref.shape[1]
    inner = w_ref.shape[1] // 2
    parts, degrees, _, part_rows, _ = table_ref.shape
    step = pl.program_id(0)

    @pl.when(step == 0)
    def _():
        def load(a, rows, lane, width):
            read = lambda start: code_ref[a, rows, pl.ds(start, width)].astype(jnp.float32)
            return (read(lane), read(inner + lane))

        first_stage(load, turn_ref, hi_ref, lo_ref, slots, inner)
        out_ref[...] = jnp.zeros_like(out_ref)

    g_ref[...] = second_stage(step, w_ref, hi_ref, lo_ref)
    width = min(128, slots)
    lanes = [pl.ds(lane, width) for lane in range(0, slots, width)]
    keys = [(j, part, at) for at in range(len(lanes)) for j in range(degrees) for part in range(2)]

    def body(i, sums):
        new = dict(zip(keys, sums))
        for source in range(parts):
            local = pl.multiple_of(i * 16, 16)
            rows = pl.multiple_of(source * part_rows + i * 16, 16)
            scale = [weight_ref[0, pl.ds(rows, 16), j : j + 1] for j in range(degrees)]
            for at in range(len(lanes)):
                g = [g_ref[pl.ds(part * inner + rows, 16), lanes[at]] for part in range(2)]
                for j in range(degrees):
                    scaled = table_ref[source, j, 0, pl.ds(local, 16), lanes[at]].astype(jnp.float32) * scale[j]
                    for part in range(2):
                        product = scaled * g[part]
                        new[j, part, at] += product[:8] + product[8:]
        return tuple(new[key] for key in keys)

    sums = tuple(out_ref[j, part, :, lanes[at]] for j, part, at in keys)
    sums = lax.fori_loop(0, part_rows // 16, body, sums, unroll=True)
    for key, total in zip(keys, sums):
        out_ref[key[0], key[1], :, lanes[key[2]]] = total


def back(code, w, turns, weights, tables):
    slots = code.shape[1]
    inner = w.shape[1] // 2
    parts, degrees = tables.shape[:2]
    vmem = pl.BlockSpec(memory_space=pltpu.VMEM)
    sums = pl.pallas_call(
        back_kernel,
        grid=(RADIX,),
        in_specs=[
            vmem,
            vmem,
            vmem,
            pl.BlockSpec((1, inner, degrees), lambda k: (k, 0, 0)),
            pl.BlockSpec((parts, degrees, 1, inner // parts, slots), lambda k: (0, 0, k, 0, 0)),
        ],
        out_specs=pl.BlockSpec((degrees, 2, 8, slots), lambda k: (0, 0, 0, 0)),
        out_shape=jax.ShapeDtypeStruct((degrees, 2, 8, slots), jnp.float32),
        scratch_shapes=[
            pltpu.VMEM((RADIX, slots, 2 * inner), jnp.bfloat16),
            pltpu.VMEM((RADIX, slots, 2 * inner), jnp.bfloat16),
            pltpu.VMEM((2 * inner, slots), jnp.float32),
        ],
        compiler_params=pltpu.CompilerParams(
            vmem_limit_bytes=VMEM_BYTES, dimension_semantics=("arbitrary",)
        ),
    )(code, w, turns, weights, tables)
    return jnp.sum(sums, axis=2)


def dft_tables(length):
    inner = length // RADIX
    place = np.arange(inner)
    angle = 2 * np.pi / inner * (place[:, None] * place[None, :] % inner)
    c, s = np.cos(angle), np.sin(angle)
    full = np.block([[c, s], [-s, c]]).astype(np.float32)
    hi = full.astype(jnp.bfloat16)
    lo = (full - hi.astype(np.float32)).astype(jnp.bfloat16)
    twist = 2 * np.pi / length * (np.arange(RADIX)[:, None] * place[None, :])
    return (
        jnp.asarray(np.stack([hi, lo])),
        jnp.asarray(np.stack([np.cos(twist), np.sin(twist)]).astype(np.float32)),
    )


def on_device(maps, deltas, spin_rows, ell_index, owner_map, prior):
    axes = ("theta", "phi")
    phi_count = lax.axis_size("phi")
    ranks = lax.axis_size("theta") * phi_count
    planes, block_rows, half_cols = maps.shape
    length = half_cols * phi_count
    inner = length // RADIX
    rows = block_rows // phi_count
    slots = length // ranks
    degrees = deltas.shape[1]
    w, turns = dft_tables(length)

    halves = lax.all_to_all(
        maps.reshape(planes, phi_count, rows, half_cols).transpose(1, 0, 2, 3),
        "phi",
        split_axis=0,
        concat_axis=0,
    )
    source_rows = jnp.mod(owner_map, RADIX) * inner + owner_map // RADIX
    received = []
    for spin in range(2):
        code = front(halves, w, turns, source_rows, spin)
        if spin == 1:
            code, deltas = lax.optimization_barrier((code, deltas))
        code = lax.all_to_all(code.reshape(ranks, slots, 2 * rows).astype(LINK_TYPE), axes, split_axis=0, concat_axis=0)
        code = code.astype(jnp.float32).reshape(RADIX, ranks // RADIX, slots, 2, rows)
        received.append(code.transpose(0, 2, 3, 1, 4).reshape(RADIX, slots, 2 * inner))

    part = inner // phi_count
    tables = deltas.reshape(part, RADIX, degrees, phi_count, slots).transpose(3, 2, 1, 0, 4)
    tables = lax.all_to_all(tables, "phi", split_axis=0, concat_axis=0)
    spin_all = lax.all_gather(spin_rows, "phi", axis=0, tiled=True).astype(jnp.float32)
    positions = jnp.arange(length, dtype=jnp.int32)
    freq = jnp.where(positions < length // 2, positions, positions - length)
    keep_rows = (jnp.abs(freq)[:, None] <= ell_index[None, :]).astype(jnp.float32)
    shares = []
    for spin in range(2):
        weights = (spin_all[:, spin] * keep_rows).reshape(inner, RADIX, degrees).transpose(1, 0, 2)
        shares.append(back(received[spin], w, turns, weights, tables))

    slot_start = (lax.axis_index("theta") * phi_count + lax.axis_index("phi")) * slots
    share_ids = lax.dynamic_slice_in_dim(owner_map, slot_start, slots)
    slot_freq = jnp.where(share_ids < length // 2, share_ids, share_ids - length)
    ell_float = ell_index.astype(jnp.float32)
    weight = 2.0 * math.pi / length * jnp.sqrt((2.0 * ell_float + 1.0) / (4.0 * math.pi)) / (length * LINK_SCALE)
    keep_slots = (jnp.abs(slot_freq)[None, :] <= ell_index[:, None]).astype(jnp.float32) * weight[
        :, None
    ]
    scalar_real = shares[0][:, 0] * keep_slots
    scalar_imag = shares[0][:, 1] * keep_slots
    spin_real = shares[1][:, 0] * keep_slots
    spin_imag = shares[1][:, 1] * keep_slots
    coupling = (prior * jnp.sqrt(ell_float * (ell_float + 1.0)) / (length // 2))[:, None]
    inner_real = -spin_imag - coupling * scalar_real
    inner_imag = spin_real - coupling * scalar_imag
    turned = jnp.mod(-slot_freq, 4)
    phase_real = jnp.where(turned == 0, 1.0, jnp.where(turned == 2, -1.0, 0.0)).astype(jnp.float32)
    phase_imag = jnp.where(turned == 1, 1.0, jnp.where(turned == 3, -1.0, 0.0)).astype(jnp.float32)
    out_real = phase_real * inner_real - phase_imag * inner_imag
    out_imag = phase_real * inner_imag + phase_imag * inner_real
    return jnp.stack([out_real, out_imag], axis=1)


def solution(mesh):
    placed = (
        P("grp", "theta", "phi"),
        P("phi", None, "theta"),
        P("phi", None, None),
        P(),
        P(),
        P(),
    )
    return jax.shard_map(
        on_device,
        mesh=mesh,
        in_specs=placed,
        out_specs=P("grp", None, ("theta", "phi")),
        check_vma=False,
    )
```

time: 1110 us -> 325 us (0.29)
  matrix products: 354 us -> 0 us
  local copies, waits for them, and re-layouts: 310 us -> 38.4 us
  other arithmetic: 161 us -> 32.3 us
  waiting for transfers between devices: 240 us -> 113 us
  Pallas kernels: 0 us -> 111 us
  starting transfers between devices: 5.84 us -> 26.2 us
  blocking collectives: 19.9 us -> 2.08 us
  between operations: 14.1 us -> 0.12 us
    dot_general x22 -> x0, matrix products: 354 us -> none  [exact_einsum(): return jnp.einsum(form, table, operand, precision=lax.Precision.HIGHEST)]
    pallas_call x0 -> x4, Pallas kernels: none -> 111 us  [the longest x2 66.7 us: front(): pl.pallas_call(functools.partial(front_kernel, spin=spin), grid=(1,), in_...]
    all_to_all x1 -> x4, waiting for transfers between devices: 213 us -> 113 us  [the longest x2 105 us: on_device(): lax.all_to_all(code.reshape(ranks, slots, 2 * rows).astype(LINK_TYPE), ax...]
    another operation x8 -> x0, local copies, waits for them, and re-layouts: 72.7 us -> none  [the longest x2 18.9 us: on_device(): jnp.stack([spectrum[0] for spectrum in spectra])]
    unnamed x68 -> x8, local copies, waits for them, and re-layouts: 68.2 us -> 0.02 us
    gather x1 -> x0, local copies, waits for them, and re-layouts: 52.5 us -> none  [on_device(): permuted = jnp.take(stacked, owner_map, axis=3)]
    another operation x6 -> x0, other arithmetic: 49.2 us -> none  [the longest x3 24 us: on_device(): jnp.stack([jnp.stack([spectrum[0] for spectrum in spectra]), jnp.stack([s...]
    unnamed x2 -> x0, other arithmetic: 40.3 us -> none
  transfers between devices with their start and end apart: 3 -> 4, of which waited for: 3 -> 4; matrix products, arithmetic and copies ran while one was open for 11% -> 9% of each run, Pallas kernels for 0% -> 17%
where the time goes in v1:
time: 325 us; the launch traced here: 323 us
  waiting for transfers between devices  113 us (35%)
  Pallas kernels  111 us (34%)
  local copies, waits for them, and re-layouts  38.4 us (12%)
  other arithmetic  32.3 us (10%)
  starting transfers between devices  26.2 us (8%)
    all_to_all x2, waiting for transfers between devices, on_device(): lax.all_to_all(code.reshape(ranks, slots, 2 * rows).astype(LINK_TYPE), ax...  105 us
    pallas_call x2, Pallas kernels, front(): pl.pallas_call(functools.partial(front_kernel, spin=spin), grid=(1,), in_...  66.7 us
    pallas_call x2, Pallas kernels, back(): pl.pallas_call(back_kernel, grid=(RADIX,), in_specs=[vmem, vmem, vmem, pl...  44.7 us
    reshape x2, local copies, waits for them, and re-layouts, on_device(): deltas.reshape(part, RADIX, degrees, phi_count, slots)  24.5 us
    convert_element_type x2, other arithmetic, on_device(): code.astype(jnp.float32).reshape(RADIX, ranks // RADIX, slots, 2, rows)  13 us
    convert_element_type x2, other arithmetic, on_device(): code.reshape(ranks, slots, 2 * rows).astype(LINK_TYPE)  12.4 us
    all_to_all x2, starting transfers between devices, on_device(): lax.all_to_all(code.reshape(ranks, slots, 2 * rows).astype(LINK_TYPE), ax...  11.1 us
    reshape x1, local copies, waits for them, and re-layouts, on_device(): maps.reshape(planes, phi_count, rows, half_cols).transpose(1, 0, 2, 3)  8.26 us
  transfers between devices with their start and end apart: 4, of which 4 were waited for; matrix products, arithmetic and copies ran while one was open for 9% of the time, Pallas kernels for 17%

profile of v1, /device:TPU:11, one launch (start us, length us, event | category | flops | bytes accessed | tf_op | source)
XLA Modules:
  0.0 323.3 jit_solution(3976807123958335991)
XLA Ops:
  0.0 8.3 %copy.19 = bf16[4,2,256,2048]{3,2,0,1:T(8,128)(2,1)} copy(bf16[4,2,256,2048]{3,2,1,0:T(8,128)(2,1)} %bitcast.21) | data formatting | bytes 16777216 | tf_op jit(solution)/shard_map/reshape | solution.py:263
  8.3 7.8 %all-to-all-start = ((bf16[2,4,256,2048]{3,2,1,0:T(8,128)(2,1)}), bf16[2,4,256,2048]{3,2,1,0:T(8,128)(2,1)}, u32[]{:S(2)}, u32[]{:S(2)}) async-start(bf16[2,4,256,2048]{3,2,1,0:T(8,128)(2,1)} %bitcast.18), calls=%async_computation | async-start | bytes 16777216 | tf_op jit(solution)/shard_map/all_to_all | solution.py:262
  16.0 0.6 fusion.3.rows_ref
  16.6 6.5 %all-to-all-done.refs_0_.refs_1_.refs_2_ = bf16[2,4,256,2048]{3,2,1,0:T(8,128)(2,1)} async-done(((bf16[2,4,256,2048]{3,2,1,0:T(8,128)(2,1)}), bf16[2,4,256,2048]{3,2,1,0:T(8,128)(2,1)}, u32[]{:S(2)}, u32[]{:S(2)}) %all-to-all-start) | async-done | bytes 8388640 | tf_op jit(solution)/shard_map/all_to_all | solution.py:262
  23.1 34.6 %shard_map.82 = f32[4096,512]{1,0:T(8,128)} custom-call(s32[4096]{0:T(1024)} %fusion.3.rows_ref, bf16[2,512,512]{2,1,0:T(8,128)(2,1)} %constant.99.clone.w_ref, f32[2,16,256]{2,1,0:T(8,128)} %constant.100.clone.turn_ref, bf16[2,4,256,2048]{3,2,1,0:T(8,128)(2,1)} %all-to-all-done.refs_0_.refs_1_.refs_2_, ...), custom_call_target="tpu_custom_call" | custom-call | tf_op jit(solution)/shard_map/pallas_call | solution.py:150
  57.8 13.1 %reshape.157 = bf16[128,16,4,2,256]{4,3,2,1,0:T(2,128)(2,1)} reshape(bf16[2048,4,512]{2,1,0:T(4,128)(2,1)} %param.9) | data formatting | bytes 16777216 | tf_op jit(solution)/shard_map/reshape | solution.py:279
  70.9 11.4 %copy.18 = bf16[128,16,4,2,256]{4,0,1,2,3:T(8,128)(2,1)} copy(bf16[128,16,4,2,256]{4,3,2,1,0:T(2,128)(2,1)} %reshape.157) | data formatting | bytes 16777216 | tf_op jit(solution)/shard_map/reshape | solution.py:279
  82.3 7.3 %all-to-all-start.2 = ((bf16[2,4,16,128,256]{4,3,2,1,0:T(8,128)(2,1)}), bf16[2,4,16,128,256]{4,3,2,1,0:T(8,128)(2,1)}, u32[]{:S(2)}, u32[]{:S(2)}) async-start(bf16[2,4,16,128,256]{4,3,2,1,0:T(8,128)(2,1)} %bitcast.17), calls=%async_computation.2 | async-start | bytes 16777216 | tf_op jit(solution)/shard_map/all_to_all | solution.py:280
  89.6 6.2 %convert_element_type.26 = f16[4096,512]{1,0:T(8,128)(2,1)} convert(f32[4096,512]{1,0:T(8,128)} %shard_map.82) | non-fusion elementwise | flops 2097152 | bytes 12582912 | tf_op jit(solution)/shard_map/convert_element_type | solution.py:274
  95.8 0.9 all-to-all-done.2.table_ref
  96.7 6.2 %all-to-all-start.1 = ((f16[16,256,512]{2,1,0:T(8,128)(2,1)}), f16[16,256,512]{2,1,0:T(8,128)(2,1)}, u32[]{:S(2)}, u32[]{:S(2)}) async-start(f16[16,256,512]{2,1,0:T(8,128)(2,1)} %bitcast.20), calls=%async_computation.1 | async-start | bytes 8388608 | tf_op jit(solution)/shard_map/all_to_all | solution.py:274
  102.9 32.1 %shard_map.84 = f32[4096,512]{1,0:T(8,128)} custom-call(s32[4096]{0:T(1024)} %fusion.3.rows_ref, bf16[2,512,512]{2,1,0:T(8,128)(2,1)} %constant.99.clone.w_ref, f32[2,16,256]{2,1,0:T(8,128)} %constant.100.clone.turn_ref, bf16[2,4,256,2048]{3,2,1,0:T(8,128)(2,1)} %all-to-all-done.refs_0_.refs_1_.refs_2_), custom_call_target="tpu_custom_call" | custom-call | tf_op jit(solution)/shard_map/pallas_call | solution.py:150
  135.1 6.1 %convert_element_type.31 = f16[4096,512]{1,0:T(8,128)(2,1)} convert(f32[4096,512]{1,0:T(8,128)} %shard_map.84) | non-fusion elementwise | flops 2097152 | bytes 12582912 | tf_op jit(solution)/shard_map/convert_element_type | solution.py:274
  141.2 54.2 %all-to-all-done.1 = f16[16,256,512]{2,1,0:T(8,128)(2,1)} async-done(((f16[16,256,512]{2,1,0:T(8,128)(2,1)}), f16[16,256,512]{2,1,0:T(8,128)(2,1)}, u32[]{:S(2)}, u32[]{:S(2)}) %all-to-all-start.1) | async-done | bytes 4194336 | tf_op jit(solution)/shard_map/all_to_all | solution.py:274
  195.4 4.9 %all-to-all-start.3 = ((f16[16,256,512]{2,1,0:T(8,128)(2,1)}), f16[16,256,512]{2,1,0:T(8,128)(2,1)}, u32[]{:S(2)}, u32[]{:S(2)}) async-start(f16[16,256,512]{2,1,0:T(8,128)(2,1)} %bitcast.19), calls=%async_computation.3 | async-start | bytes 8388608 | tf_op jit(solution)/shard_map/all_to_all | solution.py:274
  200.4 2.1 all_gather.3
  202.4 0.2 squeeze.4
  202.7 2.0 copy.10
  204.7 0.2 squeeze.5
  204.9 3.1 copy.13
  208.1 0.1 fusion.18
  208.1 0.1 compare_select_fusion.10
  208.3 3.6 %fusion = (f32[16,256,4]{2,1,0:T(8,128)}, f32[16,256,4]{2,1,0:T(8,128)}) fusion(f32[256,16,4]{2,0,1:T(8,128)S(1)} %copy.10, s32[4]{0:T(128)S(1)} %copy-done.2, s32[256,16]{0,1:T(8,128)S(1)} %fusion.4, f32[256,16,4]{2,0,1:T(8,128)} %copy.13), kind=kLoop, calls=%fused_computation.4 | loop fusion | flops 49152 | bytes 278544 | tf_op jit(solution)/shard_map/transpose | solution.py:287
  211.9 6.5 %convert_element_type.28.code_ref = f32[16,256,512]{2,1,0:T(8,128)} convert(f16[16,256,512]{2,1,0:T(8,128)(2,1)} %all-to-all-done.1) | non-fusion elementwise | flops 2097152 | bytes 12582912 | tf_op jit(solution)/shard_map/convert_element_type | solution.py:275
  218.4 22.3 %shard_map.83 = f32[4,2,8,256]{3,2,1,0:T(8,128)} custom-call(f32[16,256,512]{2,1,0:T(8,128)} %convert_element_type.28.code_ref, bf16[2,512,512]{2,1,0:T(8,128)(2,1)} %constant.99.clone.w_ref, f32[2,16,256]{2,1,0:T(8,128)} %constant.100.clone.turn_ref, f32[16,256,4]{2,1,0:T(8,128)} %get-tuple-element.16.weight_ref, ...), custom_call_target="tpu_custom_call" | custom-call | tf_op jit(solution)/shard_map/pallas_call | solution.py:211
  240.8 0.9 reduce_sum.18
  241.6 51.1 %all-to-all-done.3 = f16[16,256,512]{2,1,0:T(8,128)(2,1)} async-done(((f16[16,256,512]{2,1,0:T(8,128)(2,1)}), f16[16,256,512]{2,1,0:T(8,128)(2,1)}, u32[]{:S(2)}, u32[]{:S(2)}) %all-to-all-start.3) | async-done | bytes 4194336 | tf_op jit(solution)/shard_map/all_to_all | solution.py:274
  292.8 6.5 %convert_element_type.33.code_ref = f32[16,256,512]{2,1,0:T(8,128)} convert(f16[16,256,512]{2,1,0:T(8,128)(2,1)} %all-to-all-done.3) | non-fusion elementwise | flops 2097152 | bytes 12582912 | tf_op jit(solution)/shard_map/convert_element_type | solution.py:275
  299.3 22.4 %shard_map.85 = f32[4,2,8,256]{3,2,1,0:T(8,128)} custom-call(f32[16,256,512]{2,1,0:T(8,128)} %convert_element_type.33.code_ref, bf16[2,512,512]{2,1,0:T(8,128)(2,1)} %constant.99.clone.w_ref, f32[2,16,256]{2,1,0:T(8,128)} %constant.100.clone.turn_ref, f32[16,256,4]{2,1,0:T(8,128)} %get-tuple-element.17.weight_ref, ...), custom_call_target="tpu_custom_call" | custom-call | tf_op jit(solution)/shard_map/pallas_call | solution.py:211
  321.7 0.9 reduce_sum.19
  322.5 0.1 multiply_subtract_fusion
  322.6 0.6 pad_maximum_fusion
  (13 shorter events, 0.1 us)
Async XLA Ops:
  8.3 7.8 %copy-start.1 = (s32[4096]{0:T(1024)S(1)}, s32[4096]{0:T(1024)}, u32[]{:S(2)}) copy-start(s32[4096]{0:T(1024)} %param.12) | copy-start | bytes 49156
  8.3 14.9 %all-to-all-start = ((bf16[2,4,256,2048]{3,2,1,0:T(8,128)(2,1)}), bf16[2,4,256,2048]{3,2,1,0:T(8,128)(2,1)}, u32[]{:S(2)}, u32[]{:S(2)}) async-start(bf16[2,4,256,2048]{3,2,1,0:T(8,128)(2,1)} %bitcast.18), calls=%async_computation | async-start | bytes 16777216 | tf_op jit(solution)/shard_map/all_to_all | solution.py:262
  82.3 14.4 %all-to-all-start.2 = ((bf16[2,4,16,128,256]{4,3,2,1,0:T(8,128)(2,1)}), bf16[2,4,16,128,256]{4,3,2,1,0:T(8,128)(2,1)}, u32[]{:S(2)}, u32[]{:S(2)}) async-start(bf16[2,4,16,128,256]{4,3,2,1,0:T(8,128)(2,1)} %bitcast.17), calls=%async_computation.2 | async-start | bytes 16777216 | tf_op jit(solution)/shard_map/all_to_all | solution.py:280
  96.7 98.7 %all-to-all-start.1 = ((f16[16,256,512]{2,1,0:T(8,128)(2,1)}), f16[16,256,512]{2,1,0:T(8,128)(2,1)}, u32[]{:S(2)}, u32[]{:S(2)}) async-start(f16[16,256,512]{2,1,0:T(8,128)(2,1)} %bitcast.20), calls=%async_computation.1 | async-start | bytes 8388608 | tf_op jit(solution)/shard_map/all_to_all | solution.py:274
  195.4 4.9 %copy-start = (bf16[2048,2,4]{0,2,1:T(4,128)(2,1)S(1)}, bf16[2048,2,4]{0,2,1:T(4,128)(2,1)}, u32[]{:S(2)}) copy-start(bf16[2048,2,4]{0,2,1:T(4,128)(2,1)} %param.10) | copy-start | bytes 98308
  195.4 97.4 %all-to-all-start.3 = ((f16[16,256,512]{2,1,0:T(8,128)(2,1)}), f16[16,256,512]{2,1,0:T(8,128)(2,1)}, u32[]{:S(2)}, u32[]{:S(2)}) async-start(f16[16,256,512]{2,1,0:T(8,128)(2,1)} %bitcast.19), calls=%async_computation.3 | async-start | bytes 8388608 | tf_op jit(solution)/shard_map/all_to_all | solution.py:274
  200.3 7.9 %copy-start.2 = (s32[4]{0:T(128)S(1)}, s32[4]{0:T(128)}, u32[]{:S(2)}) copy-start(s32[4]{0:T(128)} %param.11) | copy-start | bytes 52
  200.3 7.9 %copy-start.3 = (f32[4]{0:T(128)S(1)}, f32[4]{0:T(128)}, u32[]{:S(2)}) copy-start(f32[4]{0:T(128)} %param.13) | copy-start | bytes 52
